TPU v7x, 32 devices: a whole 2x2x4 slice. The times are simulated.
32 devices in a mesh: img: 8 (over z, y), band: 4 (over x, core).
Axes of the slice: x: 2, y: 2, z: 4, core: 2. Of those that a mesh axis runs over, the one named last changes fastest.
Arguments:
- patches: bfloat16 [32, 576, 768], P('img', 'band'), may hold values from -6 to 6
- patch_mask: int32 [32, 576], P('img', 'band'), may hold values from 0 to 1, as said below
- band_first: int32 [32, 4], P('img'), may hold values from 0 to 18, as said below
- attn_gain: bfloat16 [768], replicated, may hold values from 0.5 to 1.5
- attn_shift: bfloat16 [768], replicated, may hold values from -3 to 3
- inproj_weight: bfloat16 [768, 2304], replicated, may hold values from -0.21875 to 0.21875
- inproj_bias: bfloat16 [2304], replicated, may hold values from -2 to 2
- rotary_freqs: bfloat16 [2, 12, 32], replicated, may hold values from -3 to 3
- outproj_weight: bfloat16 [768, 768], replicated, may hold values from -0.875 to 0.875
- outproj_bias: bfloat16 [768], replicated, may hold values from -2 to 2
- mlp_gain: bfloat16 [768], replicated, may hold values from 0.5 to 1.5
- mlp_shift: bfloat16 [768], replicated, may hold values from -3 to 3
- expand_weight: bfloat16 [768, 3072], replicated, may hold values from -0.21875 to 0.21875
- expand_bias: bfloat16 [3072], replicated, may hold values from -2 to 2
- reduce_weight: bfloat16 [3072, 768], replicated, may hold values from -0.109375 to 0.109375
- reduce_bias: bfloat16 [768], replicated, may hold values from -2 to 2
- cotangent: bfloat16 [32, 576, 768], P('img', 'band'), may hold values from -6 to 6
Outputs:
- block_out: bfloat16 [32, 576, 768], P('img', 'band')
- d_patches: bfloat16 [32, 576, 768], P('img', 'band')
- grad_attn_gain: float32 [768], P('img')
- grad_attn_shift: float32 [768], P('img')
- grad_inproj_weight: float32 [768, 2304], P('img')
- grad_inproj_bias: float32 [2304], P('img')
- grad_rotary_freqs: float32 [2, 12, 32], replicated
- grad_outproj_weight: float32 [768, 768], P('img')
- grad_outproj_bias: float32 [768], P('img')
- grad_mlp_gain: float32 [768], P('img')
- grad_mlp_shift: float32 [768], P('img')
- grad_expand_weight: float32 [768, 3072], P('img')
- grad_expand_bias: float32 [3072], P('img')
- grad_reduce_weight: float32 [3072, 768], P('img')
- grad_reduce_bias: float32 [768], P('img')
Inputs may be any that keep to these rules, and one draw needn't show every extreme that they name: `patch_mask`: each image has a square grid of side 24 * 7 // 12, 20 or 24, and image 0 has side 24; the grid's rows are split over the 4 bands as evenly as possible, earlier bands taking one row more; a slot of local row i and column j of band b is 1 exactly when i is under the band's row count and j under the side. `band_first`: the first patch row of each band of each image, consistent with patch_mask's row counts.
All inputs are finite; a program needn't handle non-finite values.
Results may differ from a plain program's by a relative error of at most 0.012.
The roundings to bfloat16 on the way count: a program that leaves them out, or rounds other values in their place, can miss the bound.
Values may be sent and summed in bfloat16 or wider, within the bound.
No kernel may reach another device: no remote copies, remote signals or barrier semaphores. Data moves between devices by JAX's collectives and lax.ppermute only.
A program may use at most 192 MiB of HBM per device.

v0:
```python
import jax
import jax.numpy as jnp
from jax import lax
from jax.sharding import PartitionSpec as P

GRID = 24
EPS = 1e-06
NEG = -1e30


def norm_parts(values):
    center = values - jnp.mean(values, -1, keepdims=True)
    rstd = lax.rsqrt(jnp.mean(center * center, -1, keepdims=True) + EPS)
    return (center * rstd, rstd)


def norm_back(grad, gain, xhat, rstd):
    scaled = grad * gain
    inner = jnp.mean(scaled * xhat, -1, keepdims=True)
    return rstd * (scaled - jnp.mean(scaled, -1, keepdims=True) - xhat * inner)


def turn(tensor, cosine, sine):
    half = tensor.shape[-1] // 2
    first, second = (tensor[..., :half], tensor[..., half:])
    return jnp.concatenate([first * cosine - second * sine, first * sine + second * cosine], -1)


def matrix_sum(grad):
    low = grad.astype(jnp.bfloat16)
    low = lax.psum_scatter(low, "band", scatter_dimension=1, tiled=True)
    low = lax.psum_scatter(low, "img", scatter_dimension=0, tiled=True)
    low = lax.all_gather(low, "band", axis=1, tiled=True)
    return low.astype(jnp.float32)


def local(
    patches,
    patch_mask,
    band_first,
    attn_gain,
    attn_shift,
    inproj_weight,
    inproj_bias,
    rotary_freqs,
    outproj_weight,
    outproj_bias,
    mlp_gain,
    mlp_shift,
    expand_weight,
    expand_bias,
    reduce_weight,
    reduce_bias,
    cotangent,
):
    single = jnp.float32
    low = jnp.bfloat16
    images, slots, width = patches.shape
    heads = rotary_freqs.shape[1]
    size = width // heads
    scale = size ** (-0.5)
    bands = lax.axis_size("band")
    here = lax.axis_index("band")

    def gather_image(values):
        return lax.all_to_all(values, "band", 0, 1, tiled=True)

    def spread_image(values):
        return lax.all_to_all(values, "band", 1, 0, tiled=True)

    patches = gather_image(patches)
    cotangent = gather_image(cotangent)
    mask = gather_image(patch_mask).astype(single)
    count = images // bands
    total = slots * bands
    starts = lax.dynamic_slice_in_dim(band_first, here * count, count, 0)
    row_in = jnp.arange(slots) // GRID
    rows = (starts[:, :, None] + row_in[None, None, :]).reshape(count, total).astype(single)
    cols = jnp.broadcast_to((jnp.arange(total) % GRID).astype(single)[None, :], rows.shape)
    freqs = rotary_freqs.astype(single)
    angles = rows[..., None, None] * freqs[0] + cols[..., None, None] * freqs[1]
    cosine, sine = (jnp.cos(angles), jnp.sin(angles))
    wide = patches.astype(single)
    xhat_one, rstd_one = norm_parts(wide)
    gain_one = attn_gain.astype(single)
    attn_in = (xhat_one * gain_one + attn_shift.astype(single)).astype(low)
    projected = jnp.dot(attn_in, inproj_weight, preferred_element_type=single)
    projected = projected + inproj_bias.astype(single)
    split = projected.reshape(count, total, 3, heads, size)
    query_rot = turn(split[:, :, 0], cosine, sine).astype(low)
    key_rot = turn(split[:, :, 1], cosine, sine).astype(low)
    value_low = split[:, :, 2].astype(low)
    scores = jnp.einsum("iqhd,ikhd->ihqk", query_rot, key_rot, preferred_element_type=single)
    masked = jnp.where(mask[:, None, None, :] > 0, scores * scale, NEG)
    expo = jnp.exp(masked - jnp.max(masked, -1, keepdims=True))
    probs = expo / jnp.sum(expo, -1, keepdims=True)
    probs_low = probs.astype(low)
    mix = jnp.einsum("ihqk,ikhd->iqhd", probs_low, value_low, preferred_element_type=single)
    mix = mix.reshape(count, total, width).astype(low)
    attn_out = jnp.dot(mix, outproj_weight, preferred_element_type=single)
    resid_mid = wide + attn_out + outproj_bias.astype(single)
    xhat_two, rstd_two = norm_parts(resid_mid)
    gain_two = mlp_gain.astype(single)
    mlp_in = (xhat_two * gain_two + mlp_shift.astype(single)).astype(low)
    pre_act = jnp.dot(mlp_in, expand_weight, preferred_element_type=single)
    pre_act = pre_act + expand_bias.astype(single)
    half_erf = 0.5 + 0.5 * lax.erf(pre_act * 0.5**0.5)
    hidden = (pre_act * half_erf).astype(low)
    slope = half_erf + pre_act * jnp.exp(-0.5 * pre_act * pre_act) * 0.3989422804014327
    branch = jnp.dot(hidden, reduce_weight, preferred_element_type=single)
    block_out = mask[..., None] * (resid_mid + branch + reduce_bias.astype(single))
    block_out = spread_image(block_out.astype(low))
    grad_top = cotangent.astype(single) * mask[..., None]
    grad_low = grad_top.astype(low)
    grad_reduce_weight = jnp.einsum("iqf,iqd->fd", hidden, grad_low, preferred_element_type=single)
    grad_reduce_bias = jnp.sum(grad_top, (0, 1))
    d_hidden = jnp.einsum("iqd,fd->iqf", grad_low, reduce_weight, preferred_element_type=single)
    d_pre = (d_hidden * slope).astype(low)
    grad_expand_weight = jnp.einsum("iqd,iqf->df", mlp_in, d_pre, preferred_element_type=single)
    grad_expand_bias = jnp.sum(d_pre.astype(single), (0, 1))
    d_mlp_in = jnp.einsum("iqf,df->iqd", d_pre, expand_weight, preferred_element_type=single)
    grad_mlp_gain = jnp.sum(d_mlp_in * xhat_two, (0, 1))
    grad_mlp_shift = jnp.sum(d_mlp_in, (0, 1))
    d_mid = grad_top + norm_back(d_mlp_in, gain_two, xhat_two, rstd_two)
    d_attn = d_mid.astype(low)
    grad_outproj_weight = jnp.einsum("iqe,iqd->ed", mix, d_attn, preferred_element_type=single)
    grad_outproj_bias = jnp.sum(d_attn.astype(single), (0, 1))
    d_mix = jnp.einsum("iqd,ed->iqe", d_attn, outproj_weight, preferred_element_type=single)
    d_mix = d_mix.astype(low).reshape(count, total, heads, size)
    d_values = jnp.einsum("ihqk,iqhd->ikhd", probs_low, d_mix, preferred_element_type=single)
    d_probs = jnp.einsum("iqhd,ikhd->ihqk", d_mix, value_low, preferred_element_type=single)
    inner = jnp.sum(probs * d_probs, -1, keepdims=True)
    d_scores = (probs * (d_probs - inner)).astype(low)
    d_qrot = scale * jnp.einsum("ihqk,ikhd->iqhd", d_scores, key_rot, preferred_element_type=single)
    d_krot = scale * jnp.einsum(
        "ihqk,iqhd->ikhd", d_scores, query_rot, preferred_element_type=single
    )
    half = size // 2
    slope_q = (
        d_qrot[..., half:] * query_rot[..., :half] - d_qrot[..., :half] * query_rot[..., half:]
    )
    slope_k = d_krot[..., half:] * key_rot[..., :half] - d_krot[..., :half] * key_rot[..., half:]
    d_angle = slope_q + slope_k
    grad_freqs = jnp.stack(
        [
            jnp.sum(rows[..., None, None] * d_angle, (0, 1)),
            jnp.sum(cols[..., None, None] * d_angle, (0, 1)),
        ]
    )
    d_queries = turn(d_qrot, cosine, -sine)
    d_keys = turn(d_krot, cosine, -sine)
    flat = (count, total, width)
    d_proj = jnp.concatenate(
        [d_queries.reshape(flat), d_keys.reshape(flat), d_values.reshape(flat)], -1
    ).astype(low)
    grad_inproj_weight = jnp.einsum("iqd,iqe->de", attn_in, d_proj, preferred_element_type=single)
    grad_inproj_bias = jnp.sum(d_proj.astype(single), (0, 1))
    d_attn_in = jnp.einsum("iqe,de->iqd", d_proj, inproj_weight, preferred_element_type=single)
    grad_attn_gain = jnp.sum(d_attn_in * xhat_one, (0, 1))
    grad_attn_shift = jnp.sum(d_attn_in, (0, 1))
    d_patches = d_mid + norm_back(d_attn_in, gain_one, xhat_one, rstd_one)
    d_patches = spread_image(d_patches.astype(low))
    small = (
        grad_attn_gain,
        grad_attn_shift,
        grad_inproj_bias,
        grad_outproj_bias,
        grad_mlp_gain,
        grad_mlp_shift,
        grad_expand_bias,
        grad_reduce_bias,
        grad_freqs.reshape(-1),
    )
    packed = lax.psum(jnp.concatenate(small), ("img", "band"))
    shares = lax.axis_size("img")
    mine = lax.axis_index("img")
    sums = []
    at = 0
    for piece in small:
        long = piece.shape[0]
        sums.append(packed[at : at + long])
        at += long
    freq_total = sums.pop().reshape(grad_freqs.shape)
    sums = [
        lax.dynamic_slice_in_dim(s, mine * (s.shape[0] // shares), s.shape[0] // shares)
        for s in sums
    ]
    return (
        block_out,
        d_patches,
        sums[0],
        sums[1],
        matrix_sum(grad_inproj_weight),
        sums[2],
        freq_total,
        matrix_sum(grad_outproj_weight),
        sums[3],
        sums[4],
        sums[5],
        matrix_sum(grad_expand_weight),
        sums[6],
        matrix_sum(grad_reduce_weight),
        sums[7],
    )


def solution(mesh):
    act = P("img", "band", None)
    row = P("img")
    mat = P("img", None)
    return jax.shard_map(
        local,
        mesh=mesh,
        in_specs=(act, P("img", "band"), P("img", None)) + (P(),) * 13 + (act,),
        out_specs=(act, act, row, row, mat, row, P(), mat, row, row, row, mat, row, mat, row),
        check_vma=False,
    )
```

profile of v0, /device:TPU:0, one launch (start us, length us, event | category | flops | bytes accessed | tf_op | source)
XLA Modules:
  0.0 651.7 jit_solution(12072034389343736507)
XLA Ops:
  45.8 4.6 convolution_add_fusion
  50.3 6.5 copy.68
  59.3 4.8 subtract_convert_fusion.1
  65.4 7.4 %fusion.34 = f32[12,576,576]{1,2,0:T(8,128)} fusion(bf16[576,12,32]{0,2,1:T(8,128)(2,1)S(1)} %bitcast.128, bf16[576,12,32]{0,2,1:T(8,128)(2,1)S(1)} %bitcast.130, bf16[576,12,32]{0,2,1:T(8,128)(2,1)S(1)} %bitcast.126, bf16[576,12,32]{0,2,1:T(8,128)(2,1)S(1)} %bitcast.124), kind=kOutput, calls=%fused_computation.88 | convolution fusion | flops 513146880 | bytes 17694720 | tf_op jit(solution)/shard_map/iqhd,ikhd->ihqk/dot_general | solution.py:93
  72.7 22.2 %fusion.54 = (f32[12,576]{1,0:T(8,128)}, f32[12,576,576]{1,2,0:T(8,128)}) fusion(f32[12,576,576]{1,2,0:T(8,128)} %fusion.34, pred[576]{0:T(1024)(128)(4,1)} %broadcast_compare_fusion), kind=kOutput, calls=%fused_computation.138 | output fusion | flops 23888448 | bytes 31878720 | tf_op jit(solution)/shard_map/sub | solution.py:95
  94.9 8.4 %fusion.21 = bf16[12,64,576]{2,1,0:T(8,128)(2,1)S(1)} fusion(f32[1,576,3,12,64]{1,4,3,2,0:T(8,128)} %bitcast.122, f32[12,576,576]{1,2,0:T(8,128)} %get-tuple-element.113, f32[12,576]{1,0:T(8,128)} %get-tuple-element.112), kind=kOutput, calls=%fused_computation.63 | convolution fusion | flops 518012928 | bytes 19603456 | tf_op jit(solution)/shard_map/ihqk,ikhd->iqhd/dot_general | solution.py:98
  112.8 8.9 %multiply_convert_fusion.1 = (bf16[576,3072]{1,0:T(8,128)(2,1)}, f32[576,3072]{1,0:T(8,128)}) fusion(f32[3072]{0:T(1024)} %convert_element_type.313, bf16[768,3072]{1,0:T(8,128)(2,1)} %param.29, f32[576,768]{1,0:T(8,128)} %fusion.20, f32[768]{0:T(1024)} %convert_element_type.311, f32[768]{0:T(1024)} %convert_element_type.310, f32[576]{0:T(1024)S(1)} %add_rsqrt_fusion, ...), kind=kOutput, calls=%fused_computation.18 | convolution fusion | flops 2730737664 | bytes 17127936 | tf_op jit(solution)/shard_map/dot_general | solution.py:105
  123.2 9.2 %convert_reduce_fusion = (f32[3072]{0:T(1024)}, bf16[576,3072]{1,0:T(8,128)(2,1)S(1)}) fusion(f32[576,3072]{1,0:T(8,128)} %get-tuple-element.115, f32[3072]{0:T(1024)} %convert_element_type.313, bf16[576,768]{1,0:T(8,128)(2,1)S(1)} %fusion.19, bf16[3072,768]{1,0:T(8,128)(2,1)} %param.31), kind=kOutput, calls=%fused_computation.17 | convolution fusion | flops 2740909056 | bytes 16244736 | tf_op jit(solution)/shard_map/iqd,fd->iqf/dot_general | solution.py:117
  132.4 7.6 %multiply_reduce_fusion.1 = (f32[768]{0:T(1024)}, f32[576]{0:T(1024)S(1)}, f32[576]{0:T(1024)S(1)}, f32[768]{0:T(1024)}, f32[576,768]{1,0:T(8,128)S(1)}) fusion(f32[576,768]{1,0:T(8,128)S(1)} %copy-done.1, f32[576]{0:T(1024)S(1)} %copy-done.40, f32[576]{0:T(1024)S(1)} %copy-done.32, f32[768]{0:T(1024)S(1)} %copy-done.37, ...), kind=kOutput, calls=%fused_computation.46 | convolution fusion | flops 2721887744 | bytes 11814912 | tf_op jit(solution)/shard_map/iqf,df->iqd/dot_general | solution.py:121
  151.8 15.5 %multiply_reduce_fusion = (f32[12,576]{1,0:T(8,128)S(1)}, f32[12,576,576]{1,2,0:T(8,128)}) fusion(f32[12,576,576]{1,2,0:T(8,128)} %get-tuple-element.113, f32[12,576]{1,0:T(8,128)} %get-tuple-element.112, bf16[576,12,64]{0,2,1:T(8,128)(2,1)} %bitcast.144, f32[1,576,3,12,64]{1,4,3,2,0:T(8,128)} %bitcast.123), kind=kOutput, calls=%fused_computation.2 | convolution fusion | flops 521544960 | bytes 35654656 | tf_op jit(solution)/shard_map/iqhd,ikhd->ihqk/dot_general | solution.py:131
  167.3 12.5 %multiply_convert_fusion = bf16[12,576,576]{1,2,0:T(8,128)(2,1)S(1)} fusion(f32[12,576,576]{1,2,0:T(8,128)} %get-tuple-element.118, f32[12,576]{1,0:T(8,128)S(1)} %get-tuple-element.117, f32[12,576,576]{1,2,0:T(8,128)} %get-tuple-element.113, f32[12,576]{1,0:T(8,128)S(1)} %copy-done.27), kind=kLoop, calls=%fused_computation.1 | loop fusion | flops 15925248 | bytes 39868416 | tf_op jit(solution)/shard_map/convert_element_type | solution.py:133
  186.9 6.6 %multiply_subtract_fusion.1 = (bf16[1,576,12,32]{1,3,2,0:T(8,128)(2,1)S(1)}, bf16[1,576,12,32]{1,3,2,0:T(8,128)(2,1)S(1)}, bf16[1,576,12,32]{1,3,2,0:T(8,128)(2,1)S(1)}, bf16[1,576,12,32]{1,3,2,0:T(8,128)(2,1)S(1)}) fusion(f32[1,576,12,64]{1,3,2,0:T(8,128)} %multiply_bitcast_fusion.1, f32[12,32]{1,0:T(8,128)} %get-tuple-element.111, f32[576]{0:T(1024)S(1)} %copy-done.24, ...), kind=kLoop, calls=%fused_computation.78 | loop fusion | flops 4423680 | bytes 5316096 | tf_op jit(solution)/shard_map/sub | solution.py:26
  195.1 9.5 %fusion.24 = bf16[12,64,576]{2,1,0:T(8,128)(2,1)S(1)} fusion(bf16[576,12,64]{0,2,1:T(8,128)(2,1)S(1)} %bitcast.145, f32[12,576,576]{1,2,0:T(8,128)} %get-tuple-element.113, f32[12,576]{1,0:T(8,128)S(1)} %copy-done.28), kind=kOutput, calls=%fused_computation.64 | convolution fusion | flops 518012928 | bytes 17722368 | tf_op jit(solution)/shard_map/ihqk,iqhd->ikhd/dot_general | solution.py:130
  205.6 7.2 %convolution_convert_fusion = bf16[768,2304]{0,1:T(8,128)(2,1)} fusion(bf16[576,768]{0,1:T(8,128)(2,1)S(1)} %bitcast.146, bf16[576,768]{0,1:T(8,128)(2,1)S(1)} %bitcast.141, bf16[576,768]{0,1:T(8,128)(2,1)S(1)} %bitcast.138, f32[576,768]{1,0:T(8,128)S(1)} %copy-done.16, f32[768]{0:T(1024)S(1)} %copy-done.43, f32[768]{0:T(1024)S(1)} %copy-done.35), kind=kOutput, calls=%fused_computation.21 | convolution fusion | flops 2049490944 | bytes 7968768 | tf_op jit(solution)/shard_map/iqd,iqe->de/dot_general | solution.py:156
  213.0 8.3 %convolution_convert_fusion.1 = bf16[3072,768]{0,1:T(8,128)(2,1)} fusion(bf16[576,3072]{1,0:T(8,128)(2,1)} %get-tuple-element.114, bf16[576,768]{1,0:T(8,128)(2,1)} %copy-done.20), kind=kOutput, calls=%fused_computation.22 | convolution fusion | flops 2720268288 | bytes 9142272 | tf_op jit(solution)/shard_map/iqf,iqd->fd/dot_general | solution.py:115
  222.1 9.2 %convolution_convert_fusion.2 = bf16[768,3072]{1,0:T(8,128)(2,1)} fusion(bf16[576,3072]{1,0:T(8,128)(2,1)} %copy-done.50, f32[576,768]{1,0:T(8,128)} %fusion.20, f32[768]{0:T(1024)} %convert_element_type.311, f32[768]{0:T(1024)S(1)} %copy-done.38, f32[576]{0:T(1024)} %copy-done.39, f32[576]{0:T(1024)S(1)} %copy-done.33), kind=kOutput, calls=%fused_computation.23 | convolution fusion | flops 2722480128 | bytes 10037760 | tf_op jit(solution)/shard_map/iqd,iqf->df/dot_general | solution.py:119
  233.4 24.4 %reduce-scatter.15.cloned.1.call-done = bf16[768,576]{0,1:T(8,128)(2,1)} async-done(((bf16[768,2304]{0,1:T(8,128)(2,1)}), bf16[768,576]{0,1:T(8,128)(2,1)}) %reduce-scatter.15.cloned.1.call-update) | async-done | bytes 884752 | tf_op jit(solution)/shard_map/reduce_scatter | solution.py:31
  260.3 48.0 %reduce-scatter.23.cloned.1.call-done = bf16[3072,192]{0,1:T(8,128)(2,1)} async-done(((bf16[3072,768]{0,1:T(8,128)(2,1)}), bf16[3072,192]{0,1:T(8,128)(2,1)}) %reduce-scatter.23.cloned.1.call-update) | async-done | bytes 1179664 | tf_op jit(solution)/shard_map/reduce_scatter | solution.py:31
  310.8 6.8 %fusion.27 = bf16[1,576,768]{2,1,0:T(8,128)(2,1)S(1)} fusion(f32[576,768]{1,0:T(8,128)} %fusion.20, bf16[576,3072]{1,0:T(8,128)(2,1)} %get-tuple-element.114, bf16[3072,768]{1,0:T(8,128)(2,1)} %param.31, f32[768]{0:T(1024)S(1)} %convert_element_type.315, f32[576]{0:T(1024)S(1)} %convert_element_type.290), kind=kOutput, calls=%fused_computation.67 | convolution fusion | flops 2719678464 | bytes 10917120 | tf_op jit(solution)/shard_map/dot_general | solution.py:110
  320.8 8.0 %reduce.39 = bf16[576,768]{1,0:T(8,128)(2,1)} reduce(bf16[576,1,768]{2,1,0:T(2,128)(2,1)} %bitcast.134, bf16[]{:T(256)} %broadcast.353), dimensions={1}, to_apply=%bitcast.118.reduce_sub_computation | reduce | bytes 1769474
  336.8 6.8 %fusion.52 = (f32[768]{0:T(1024)S(1)}, f32[768]{0:T(1024)S(1)}, f32[576]{0:T(1024)S(1)}, f32[576]{0:T(1024)S(1)}, f32[576,768]{1,0:T(8,128)}) fusion(f32[576]{0:T(1024)S(1)} %copy-done.30, f32[576]{0:T(1024)S(1)} %copy-done.23, bf16[4,144,768]{2,1,0:T(8,128)(2,1)} %all-to-all-done.1, f32[576,768]{1,0:T(8,128)} %copy-done.15, ...), kind=kOutput, calls=%fused_computation.136 | convolution fusion | flops 2050815488 | bytes 10635264 | tf_op jit(solution)/shard_map/iqe,de->iqd/dot_general | solution.py:158
  348.6 19.5 %reduce-scatter.19.cloned.1.call-done = bf16[768,768]{1,0:T(8,128)(2,1)} async-done(((bf16[768,3072]{1,0:T(8,128)(2,1)}), bf16[768,768]{1,0:T(8,128)(2,1)}) %reduce-scatter.19.cloned.1.call-update) | async-done | bytes 1179664 | tf_op jit(solution)/shard_map/reduce_scatter | solution.py:31
  376.2 7.9 %reduce.40 = bf16[576,768]{1,0:T(8,128)(2,1)} reduce(bf16[576,1,768]{2,1,0:T(2,128)(2,1)} %bitcast.135, bf16[]{:T(256)} %broadcast.353), dimensions={1}, to_apply=%bitcast.117.reduce_sub_computation | reduce | bytes 1769474
  394.0 4.5 all-to-all-start.4
  404.8 41.6 %psum.7 = f32[10752]{0:T(1024)} all-reduce(f32[10752]{0:T(1024)} %constant_dynamic-update-slice_fusion), channel_id=1, replica_groups=mesh['img'=8,'band'=4] {'img','band'}, use_global_device_ids=true, to_apply=%region_21.22 | all-reduce | flops 10752 | bytes 86016 | tf_op jit(solution)/shard_map/psum | solution.py:174
  472.2 7.9 %all_gather.13 = bf16[96,768]{0,1:T(8,128)(2,1)} all-gather(bf16[96,192]{0,1:T(8,128)(2,1)} %copy.89), channel_id=1, replica_groups=mesh['img'=8,'band'=4] {'band'}, dimensions={1}, use_global_device_ids=true | all-gather | bytes 184320 | tf_op jit(solution)/shard_map/all_gather | solution.py:33
  481.9 18.5 %reduce-scatter.25.cloned.1.call-done = bf16[96,576]{1,0:T(8,128)(2,1)} async-done(((bf16[768,576]{1,0:T(8,128)(2,1)}), bf16[96,576]{1,0:T(8,128)(2,1)}) %reduce-scatter.25.cloned.1.call-update) | async-done | bytes 110608
  503.8 7.2 %all-gather = bf16[4,576,96]{1,2,0:T(8,128)(2,1)S(1)} all-gather(bf16[1,576,96]{1,2,0:T(8,128)(2,1)} %copy.77), channel_id=1, replica_groups=mesh['img'=8,'band'=4] {'band'}, dimensions={0}, use_global_device_ids=true | all-gather | bytes 552960 | tf_op jit(solution)/shard_map/all_gather | solution.py:33
  514.9 53.6 %reduce-scatter.29.cloned.1.call-done = bf16[384,192]{1,0:T(8,128)(2,1)} async-done(((bf16[3072,192]{1,0:T(8,128)(2,1)}), bf16[384,192]{1,0:T(8,128)(2,1)}) %reduce-scatter.29.cloned.1.call-update) | async-done | bytes 147472
  570.2 8.4 %all_gather.15 = bf16[384,768]{0,1:T(8,128)(2,1)} all-gather(bf16[384,192]{0,1:T(8,128)(2,1)} %copy.91), channel_id=1, replica_groups=mesh['img'=8,'band'=4] {'band'}, dimensions={1}, use_global_device_ids=true | all-gather | bytes 737280 | tf_op jit(solution)/shard_map/all_gather | solution.py:33
  580.8 54.7 %reduce-scatter.21.cloned.1.call-done = bf16[96,768]{1,0:T(8,128)(2,1)} async-done(((bf16[768,768]{1,0:T(8,128)(2,1)}), bf16[96,768]{1,0:T(8,128)(2,1)}) %reduce-scatter.21.cloned.1.call-update) | async-done | bytes 147472 | tf_op jit(solution)/shard_map/reduce_scatter | solution.py:32
  635.5 7.7 %all_gather.14 = bf16[96,3072]{1,0:T(8,128)(2,1)S(1)} all-gather(bf16[96,768]{1,0:T(8,128)(2,1)} %reduce-scatter.21.cloned.1.call-done), channel_id=1, replica_groups=mesh['img'=8,'band'=4] {'band'}, dimensions={1}, use_global_device_ids=true | all-gather | bytes 737280 | tf_op jit(solution)/shard_map/all_gather | solution.py:33
  (227 shorter events, 162.6 us)
Async XLA Ops:
  7.2 38.6 %copy-start = (bf16[768,2304]{1,0:T(8,128)(2,1)S(1)}, bf16[768,2304]{1,0:T(8,128)(2,1)}, u32[]{:S(2)}) copy-start(bf16[768,2304]{1,0:T(8,128)(2,1)} %param.22) | copy-start | bytes 10616836
  8.6 8.0 %all-to-all-start = ((s32[4,1,144]{2,1,0:T(1,128)}), s32[4,1,144]{2,1,0:T(1,128)S(1)}, u32[]{:S(2)}, u32[]{:S(2)}) async-start(s32[4,1,144]{2,1,0:T(1,128)} %all_to_all.17), calls=%async_computation | async-start | bytes 8192 | tf_op jit(solution)/shard_map/all_to_all | solution.py:66
  16.7 17.0 %all-to-all-start.1 = ((bf16[4,144,768]{2,1,0:T(8,128)(2,1)}), bf16[4,144,768]{2,1,0:T(8,128)(2,1)}, u32[]{:S(2)}, u32[]{:S(2)}) async-start(bf16[4,144,768]{2,1,0:T(8,128)(2,1)} %param.17), calls=%async_computation.1 | async-start | bytes 1769472 | tf_op jit(solution)/shard_map/all_to_all | solution.py:66
  33.7 88.0 %all-to-all-start.3 = ((bf16[4,144,768]{2,1,0:T(8,128)(2,1)}), bf16[4,144,768]{2,1,0:T(8,128)(2,1)}, u32[]{:S(2)}, u32[]{:S(2)}) async-start(bf16[4,144,768]{2,1,0:T(8,128)(2,1)} %param.33), calls=%async_computation.3 | async-start | bytes 1769472 | tf_op jit(solution)/shard_map/all_to_all | solution.py:66
  37.9 193.4 %reduce-scatter.17.cloned.1.call-start = ((), (), s32[]{:S(2)}) async-start(), calls=%async_computation.14 | async-start | bytes 1474560 | tf_op jit(solution)/shard_map/reduce_scatter | solution.py:31
  94.9 9.3 %copy-start.44 = (f32[768]{0:T(1024)S(1)}, f32[768]{0:T(1024)}, u32[]{:S(2)}) copy-start(f32[768]{0:T(1024)} %convert_element_type.309) | copy-start | bytes 9220
  94.9 9.3 %copy-start.47 = (bf16[768,768]{1,0:T(8,128)(2,1)S(1)}, bf16[768,768]{1,0:T(8,128)(2,1)}, u32[]{:S(2)}) copy-start(bf16[768,768]{1,0:T(8,128)(2,1)} %param.25) | copy-start | bytes 3538948
  123.1 9.2 %copy-start.20 = (bf16[576,768]{1,0:T(8,128)(2,1)}, bf16[576,768]{1,0:T(8,128)(2,1)S(1)}, u32[]{:S(2)}) copy-start(bf16[576,768]{1,0:T(8,128)(2,1)S(1)} %fusion.19) | copy-start | bytes 2654212
  123.1 9.2 %copy-start.1 = (f32[576,768]{1,0:T(8,128)S(1)}, f32[576,768]{1,0:T(8,128)}, u32[]{:S(2)}) copy-start(f32[576,768]{1,0:T(8,128)} %fusion.20) | copy-start | bytes 5308420
  151.8 15.5 %copy-start.27 = (f32[12,576]{1,0:T(8,128)S(1)}, f32[12,576]{1,0:T(8,128)}, u32[]{:S(2)}) copy-start(f32[12,576]{1,0:T(8,128)} %get-tuple-element.112) | copy-start | bytes 82948
  167.3 12.5 %copy-start.3 = (bf16[1,576,12,32]{1,3,2,0:T(8,128)(2,1)S(1)}, bf16[1,576,12,32]{1,3,2,0:T(8,128)(2,1)}, u32[]{:S(2)}) copy-start(bf16[1,576,12,32]{1,3,2,0:T(8,128)(2,1)} %copy-done.2) | copy-start | bytes 1327108
  167.3 12.6 %copy-start.5 = (bf16[1,576,12,32]{1,3,2,0:T(8,128)(2,1)S(1)}, bf16[1,576,12,32]{1,3,2,0:T(8,128)(2,1)}, u32[]{:S(2)}) copy-start(bf16[1,576,12,32]{1,3,2,0:T(8,128)(2,1)} %copy-done.4) | copy-start | bytes 1327108
  186.9 70.9 %reduce-scatter.15.cloned.1.call-start = ((), (), s32[]{:S(2)}) async-start(), calls=%async_computation.13 | async-start | bytes 4423680 | tf_op jit(solution)/shard_map/reduce_scatter | solution.py:31
  193.6 11.0 %copy-start.11 = (bf16[1,576,12,64]{1,3,2,0:T(8,128)(2,1)}, bf16[1,576,12,64]{1,3,2,0:T(8,128)(2,1)S(1)}, u32[]{:S(2)}) copy-start(bf16[1,576,12,64]{1,3,2,0:T(8,128)(2,1)S(1)} %maximum_convert_fusion) | copy-start | bytes 2654212
  195.1 9.5 %copy-start.13 = (bf16[1,576,12,64]{1,3,2,0:T(8,128)(2,1)}, bf16[1,576,12,64]{1,3,2,0:T(8,128)(2,1)S(1)}, u32[]{:S(2)}) copy-start(bf16[1,576,12,64]{1,3,2,0:T(8,128)(2,1)S(1)} %maximum_convert_fusion.1) | copy-start | bytes 2654212
  195.1 10.5 %copy-start.16 = (f32[576,768]{1,0:T(8,128)S(1)}, f32[576,768]{1,0:T(8,128)}, u32[]{:S(2)}) copy-start(f32[576,768]{1,0:T(8,128)} %copy-done.15) | copy-start | bytes 5308420
  195.1 10.5 %copy-start.35 = (f32[768]{0:T(1024)S(1)}, f32[768]{0:T(1024)}, u32[]{:S(2)}) copy-start(f32[768]{0:T(1024)} %convert_element_type.296) | copy-start | bytes 9220
  195.1 10.4 %copy-start.43 = (f32[768]{0:T(1024)S(1)}, f32[768]{0:T(1024)}, u32[]{:S(2)}) copy-start(f32[768]{0:T(1024)} %convert_element_type.297) | copy-start | bytes 9220
  212.8 95.5 %reduce-scatter.23.cloned.1.call-start = ((), (), s32[]{:S(2)}) async-start(), calls=%async_computation.17 | async-start | bytes 5898240 | tf_op jit(solution)/shard_map/reduce_scatter | solution.py:31
  221.4 146.7 %reduce-scatter.19.cloned.1.call-start = ((), (), s32[]{:S(2)}) async-start(), calls=%async_computation.15 | async-start | bytes 5898240 | tf_op jit(solution)/shard_map/reduce_scatter | solution.py:31
  231.3 29.0 %copy-start.46 = (bf16[768]{0:T(1024)(128)(2,1)S(1)}, bf16[768]{0:T(1024)(128)(2,1)}, u32[]{:S(2)}) copy-start(bf16[768]{0:T(1024)(128)(2,1)} %param.32) | copy-start | bytes 4612
  231.3 239.4 %reduce-scatter.27.cloned.1.call-start = ((), (), s32[]{:S(2)}) async-start(), calls=%async_computation.19 | async-start | bytes 442368
  233.3 267.1 %reduce-scatter.25.cloned.1.call-start = ((), (), s32[]{:S(2)}) async-start(), calls=%async_computation.18 | async-start | bytes 1105920
  260.0 308.4 %reduce-scatter.29.cloned.1.call-start = ((), (), s32[]{:S(2)}) async-start(), calls=%async_computation.20 | async-start | bytes 1769472
  332.3 61.7 %all-to-all-start.2 = ((bf16[4,2,55296]{2,1,0:T(2,128)(2,1)}), bf16[4,2,55296]{2,1,0:T(2,128)(2,1)}, u32[]{:S(2)}, u32[]{:S(2)}) async-start(bf16[4,2,55296]{2,1,0:T(2,128)(2,1)} %reshape.788), calls=%async_computation.2 | async-start | bytes 1769472 | tf_op jit(solution)/shard_map/all_to_all | solution.py:69
  336.5 299.0 %reduce-scatter.21.cloned.1.call-start = ((), (), s32[]{:S(2)}) async-start(), calls=%async_computation.16 | async-start | bytes 1327104 | tf_op jit(solution)/shard_map/reduce_scatter | solution.py:32
  336.8 9.4 %copy-start.12 = (bf16[1,576,12,64]{1,3,2,0:T(8,128)(2,1)S(1)}, bf16[1,576,12,64]{1,3,2,0:T(8,128)(2,1)}, u32[]{:S(2)}) copy-start(bf16[1,576,12,64]{1,3,2,0:T(8,128)(2,1)} %copy-done.11) | copy-start | bytes 2654212
  336.8 9.4 %copy-start.14 = (bf16[1,576,12,64]{1,3,2,0:T(8,128)(2,1)S(1)}, bf16[1,576,12,64]{1,3,2,0:T(8,128)(2,1)}, u32[]{:S(2)}) copy-start(bf16[1,576,12,64]{1,3,2,0:T(8,128)(2,1)} %copy-done.13) | copy-start | bytes 2654212
  336.8 9.4 %copy-start.19 = (bf16[12,64,576]{2,1,0:T(8,128)(2,1)S(1)}, bf16[12,64,576]{2,1,0:T(8,128)(2,1)}, u32[]{:S(2)}) copy-start(bf16[12,64,576]{2,1,0:T(8,128)(2,1)} %copy-done.18) | copy-start | bytes 2654212
  376.2 12.6 %copy-start.45 = (f32[768]{0:T(1024)S(1)}, f32[768]{0:T(1024)}, u32[]{:S(2)}) copy-start(f32[768]{0:T(1024)} %get-tuple-element.80) | copy-start | bytes 9220
  376.2 13.9 %copy-start.26 = (f32[576]{0:T(1024)S(1)}, f32[576]{0:T(1024)}, u32[]{:S(2)}) copy-start(f32[576]{0:T(1024)} %get-tuple-element.123) | copy-start | bytes 6916
  394.0 70.3 %all-to-all-start.4 = ((bf16[4,2,55296]{2,1,0:T(2,128)(2,1)}), bf16[4,2,55296]{2,1,0:T(2,128)(2,1)}, u32[]{:S(2)}, u32[]{:S(2)}) async-start(bf16[4,2,55296]{2,1,0:T(2,128)(2,1)} %reshape.790), calls=%async_computation.4 | async-start | bytes 1769472 | tf_op jit(solution)/shard_map/all_to_all | solution.py:69
  (32 other events, 102.0 us)
Sparse Core Ops, SparseCore 0:
  187.0 27.7 reduce-scatter.16
  217.4 40.3 reduce-scatter.14
  260.3 47.9 reduce-scatter.22
  310.7 57.2 reduce-scatter.18
  371.1 62.2 reduce-scatter.26
  437.2 63.1 reduce-scatter.24
  503.8 64.5 reduce-scatter.28
  571.9 63.6 reduce-scatter.20
where the time goes:
time: 658 us; the launch traced here: 652 us
  waiting for transfers between devices  220 us (33%)
  matrix products  125 us (19%)
  other arithmetic  99.8 us (15%)
  local copies, waits for them, and re-layouts  95.8 us (15%)
  blocking collectives  72.8 us (11%)
  starting transfers between devices  22.4 us (3%)
  between operations  15.3 us (2%)
    reduce_scatter x4, waiting for transfers between devices, matrix_sum(): low = lax.psum_scatter(low, 'band', scatter_dimension=1, tiled=True)  91.9 us
    unnamed x11, waiting for transfers between devices  72.2 us
    unnamed x127, local copies, waits for them, and re-layouts  57.3 us
    reduce_scatter x1, waiting for transfers between devices, matrix_sum(): low = lax.psum_scatter(low, 'img', scatter_dimension=0, tiled=True)  54.7 us
    psum x1, blocking collectives, local(): packed = lax.psum(jnp.concatenate(small), ('img', 'band'))  41.6 us
    all_gather x4, blocking collectives, matrix_sum(): low = lax.all_gather(low, 'band', axis=1, tiled=True)  31.2 us
    sub x1, other arithmetic, local(): expo = jnp.exp(masked - jnp.max(masked, -1, keepdims=True))  22.2 us
    unnamed x3, other arithmetic  16 us
  transfers between devices with their start and end apart: 13, of which 7 were waited for; matrix products, arithmetic and copies ran while one was open for 38% of the time, Pallas kernels for 0%

commit v1 on v0

--- a/solution.py
+++ b/solution.py
@@ -30,7 +30,26 @@
     low = grad.astype(jnp.bfloat16)
     low = lax.psum_scatter(low, "band", scatter_dimension=1, tiled=True)
     low = lax.psum_scatter(low, "img", scatter_dimension=0, tiled=True)
-    low = lax.all_gather(low, "band", axis=1, tiled=True)
+    val2, spare, base_arr = (lax.axis_size("band"), lax.axis_index("band"), low.shape[1])
+    column = [(dev_i, (dev_i + 1) % val2) for dev_i in range(val2)]
+    lanes = [(dev_i, (dev_i - 1) % val2) for dev_i in range(val2)]
+    answer = jnp.zeros((*low.shape[:1], val2 * base_arr, *low.shape[1 + 1 :]), low.dtype)
+    answer = lax.dynamic_update_slice_in_dim(answer, low, spare * base_arr, axis=1)
+    y_new = r_now = low
+    local_out = val2 // 2
+    j = 1
+    while j < local_out + 1:
+        y_new = lax.ppermute(y_new, axis_name="band", perm=column)
+        answer = lax.dynamic_update_slice_in_dim(
+            answer, y_new, (spare - j) % val2 * base_arr, axis=1
+        )
+        if j < val2 - local_out:
+            r_now = lax.ppermute(r_now, "band", perm=lanes)
+            answer = lax.dynamic_update_slice_in_dim(
+                answer, r_now, (spare + j) % val2 * base_arr, axis=1
+            )
+        j += 1
+    low = answer
     return low.astype(jnp.float32)
 
 

time: 658 us -> 736 us (1.12)
  waiting for transfers between devices: 220 us -> 272 us
  local copies, waits for them, and re-layouts: 95.8 us -> 137 us
  blocking collectives: 72.8 us -> 41.3 us
  other arithmetic: 99.8 us -> 109 us
  starting transfers between devices: 22.4 us -> 29.9 us
    reduce_scatter x1 -> x4, waiting for transfers between devices: 54.7 us -> 177 us  [matrix_sum(): low = lax.psum_scatter(low, 'img', scatter_dimension=0, tiled=True)]
    unnamed x11 -> x8, waiting for transfers between devices: 72.2 us -> 0.13 us
    dynamic_update_slice x0 -> x16, local copies, waits for them, and re-layouts: none -> 32.6 us  [the longest x8 16.2 us: matrix_sum(): lax.dynamic_update_slice_in_dim(answer, y_new, (spare - j) % val2 * base_...]
    all_gather x4 -> x0, blocking collectives: 31.2 us -> none  [matrix_sum(): low = lax.all_gather(low, 'band', axis=1, tiled=True)]
    ppermute x0 -> x9, local copies, waits for them, and re-layouts: none -> 14.8 us  [the longest x6 9.85 us: matrix_sum(): y_new = lax.ppermute(y_new, axis_name='band', perm=column)]
    unnamed x127 -> x128, local copies, waits for them, and re-layouts: 57.3 us -> 51.3 us
  transfers between devices with their start and end apart: 13 -> 25, of which waited for: 7 -> 8; matrix products, arithmetic and copies ran while one was open for 38% -> 40% of each run, Pallas kernels for 0% -> 0%
where the time goes in v1:
time: 736 us; the launch traced here: 729 us
  waiting for transfers between devices  272 us (37%)
  local copies, waits for them, and re-layouts  137 us (19%)
  matrix products  125 us (17%)
  other arithmetic  109 us (15%)
  blocking collectives  41.3 us (6%)
  starting transfers between devices  29.9 us (4%)
  between operations  15.2 us (2%)
    reduce_scatter x4, waiting for transfers between devices, matrix_sum(): low = lax.psum_scatter(low, 'img', scatter_dimension=0, tiled=True)  177 us
    reduce_scatter x4, waiting for transfers between devices, matrix_sum(): low = lax.psum_scatter(low, 'band', scatter_dimension=1, tiled=True)  93.5 us
    unnamed x128, local copies, waits for them, and re-layouts  51.3 us
    psum x1, blocking collectives, local(): packed = lax.psum(jnp.concatenate(small), ('img', 'band'))  41.3 us
    sub x1, other arithmetic, local(): expo = jnp.exp(masked - jnp.max(masked, -1, keepdims=True))  22.2 us
    dynamic_update_slice x8, local copies, waits for them, and re-layouts, matrix_sum(): lax.dynamic_update_slice_in_dim(answer, y_new, (spare - j) % val2 * base_...  16.2 us
    unnamed x3, other arithmetic  15.9 us
    dot_general x1, matrix products, local(): jnp.einsum('iqhd,ikhd->ihqk', d_mix, value_low, preferred_element_type=si...  15.5 us
  transfers between devices with their start and end apart: 25, of which 8 were waited for; matrix products, arithmetic and copies ran while one was open for 40% of the time, Pallas kernels for 0%

profile of v1, /device:TPU:0, one launch (start us, length us, event | category | flops | bytes accessed | tf_op | source)
XLA Modules:
  0.0 728.7 jit_solution(13120359761600922291)
XLA Ops:
  8.6 4.2 all-to-all-start
  33.7 4.2 all-to-all-start.3
  45.7 4.6 convolution_add_fusion
  50.3 6.6 copy.95
  59.4 4.8 subtract_convert_fusion.1
  65.4 7.4 %fusion.34 = f32[12,576,576]{1,2,0:T(8,128)} fusion(bf16[576,12,32]{0,2,1:T(8,128)(2,1)S(1)} %bitcast.122, bf16[576,12,32]{0,2,1:T(8,128)(2,1)S(1)} %bitcast.124, bf16[576,12,32]{0,2,1:T(8,128)(2,1)S(1)} %bitcast.120, bf16[576,12,32]{0,2,1:T(8,128)(2,1)S(1)} %bitcast.118), kind=kOutput, calls=%fused_computation.88 | convolution fusion | flops 513146880 | bytes 17694720 | tf_op jit(solution)/shard_map/iqhd,ikhd->ihqk/dot_general | solution.py:112
  72.8 22.2 %fusion.55 = (f32[12,576]{1,0:T(8,128)}, f32[12,576,576]{1,2,0:T(8,128)}) fusion(f32[12,576,576]{1,2,0:T(8,128)} %fusion.34, pred[576]{0:T(1024)(128)(4,1)} %broadcast_compare_fusion), kind=kOutput, calls=%fused_computation.143 | output fusion | flops 23888448 | bytes 31878720 | tf_op jit(solution)/shard_map/sub | solution.py:114
  95.0 8.4 %fusion.21 = bf16[12,64,576]{2,1,0:T(8,128)(2,1)S(1)} fusion(f32[1,576,3,12,64]{1,4,3,2,0:T(8,128)} %bitcast.116, f32[12,576,576]{1,2,0:T(8,128)} %get-tuple-element.98, f32[12,576]{1,0:T(8,128)} %get-tuple-element.97), kind=kOutput, calls=%fused_computation.63 | convolution fusion | flops 518012928 | bytes 19603456 | tf_op jit(solution)/shard_map/ihqk,ikhd->iqhd/dot_general | solution.py:117
  112.9 8.9 %multiply_convert_fusion.1 = (bf16[576,3072]{1,0:T(8,128)(2,1)}, f32[576,3072]{1,0:T(8,128)}) fusion(f32[3072]{0:T(1024)} %convert_element_type.313, bf16[768,3072]{1,0:T(8,128)(2,1)} %param.29, f32[576,768]{1,0:T(8,128)} %fusion.20, f32[768]{0:T(1024)} %convert_element_type.311, f32[768]{0:T(1024)} %convert_element_type.310, f32[576]{0:T(1024)S(1)} %add_rsqrt_fusion, ...), kind=kOutput, calls=%fused_computation.18 | convolution fusion | flops 2730737664 | bytes 17127936 | tf_op jit(solution)/shard_map/dot_general | solution.py:124
  123.3 9.3 %convert_reduce_fusion = (f32[3072]{0:T(1024)}, bf16[576,3072]{1,0:T(8,128)(2,1)S(1)}) fusion(f32[576,3072]{1,0:T(8,128)} %get-tuple-element.100, f32[3072]{0:T(1024)} %convert_element_type.313, bf16[576,768]{1,0:T(8,128)(2,1)S(1)} %fusion.19, bf16[3072,768]{1,0:T(8,128)(2,1)} %param.31), kind=kOutput, calls=%fused_computation.17 | convolution fusion | flops 2740909056 | bytes 16244736 | tf_op jit(solution)/shard_map/iqd,fd->iqf/dot_general | solution.py:136
  132.6 7.6 %multiply_reduce_fusion.1 = (f32[768]{0:T(1024)}, f32[576]{0:T(1024)S(1)}, f32[576]{0:T(1024)S(1)}, f32[768]{0:T(1024)}, f32[576,768]{1,0:T(8,128)S(1)}) fusion(f32[576,768]{1,0:T(8,128)S(1)} %copy-done.1, f32[576]{0:T(1024)S(1)} %copy-done.42, f32[576]{0:T(1024)S(1)} %copy-done.33, f32[768]{0:T(1024)S(1)} %copy-done.39, ...), kind=kOutput, calls=%fused_computation.46 | convolution fusion | flops 2721887744 | bytes 11814912 | tf_op jit(solution)/shard_map/iqf,df->iqd/dot_general | solution.py:140
  152.0 15.5 %multiply_reduce_fusion = (f32[12,576]{1,0:T(8,128)S(1)}, f32[12,576,576]{1,2,0:T(8,128)}) fusion(f32[12,576,576]{1,2,0:T(8,128)} %get-tuple-element.98, f32[12,576]{1,0:T(8,128)} %get-tuple-element.97, bf16[576,12,64]{0,2,1:T(8,128)(2,1)} %bitcast.138, f32[1,576,3,12,64]{1,4,3,2,0:T(8,128)} %bitcast.117), kind=kOutput, calls=%fused_computation.2 | convolution fusion | flops 521544960 | bytes 35654656 | tf_op jit(solution)/shard_map/iqhd,ikhd->ihqk/dot_general | solution.py:150
  167.5 12.2 %multiply_convert_fusion = bf16[12,576,576]{1,2,0:T(8,128)(2,1)S(1)} fusion(f32[12,576,576]{1,2,0:T(8,128)} %get-tuple-element.103, f32[12,576]{1,0:T(8,128)S(1)} %get-tuple-element.102, f32[12,576,576]{1,2,0:T(8,128)} %get-tuple-element.98, f32[12,576]{1,0:T(8,128)S(1)} %copy-done.28), kind=kLoop, calls=%fused_computation.1 | loop fusion | flops 15925248 | bytes 39868416 | tf_op jit(solution)/shard_map/convert_element_type | solution.py:152
  186.9 6.6 multiply_subtract_fusion.1
  195.1 9.5 %fusion.24 = bf16[12,64,576]{2,1,0:T(8,128)(2,1)S(1)} fusion(bf16[576,12,64]{0,2,1:T(8,128)(2,1)S(1)} %bitcast.139, f32[12,576,576]{1,2,0:T(8,128)} %get-tuple-element.98, f32[12,576]{1,0:T(8,128)S(1)} %copy-done.29), kind=kOutput, calls=%fused_computation.64 | convolution fusion | flops 518012928 | bytes 17722368 | tf_op jit(solution)/shard_map/ihqk,iqhd->ikhd/dot_general | solution.py:149
  205.5 7.3 convolution_convert_fusion
  213.1 8.3 %convolution_convert_fusion.1 = bf16[3072,768]{0,1:T(8,128)(2,1)} fusion(bf16[576,3072]{1,0:T(8,128)(2,1)} %get-tuple-element.99, bf16[576,768]{1,0:T(8,128)(2,1)} %copy-done.20), kind=kOutput, calls=%fused_computation.22 | convolution fusion | flops 2720268288 | bytes 9142272 | tf_op jit(solution)/shard_map/iqf,iqd->fd/dot_general | solution.py:134
  222.1 9.2 %convolution_convert_fusion.2 = bf16[768,3072]{1,0:T(8,128)(2,1)} fusion(bf16[576,3072]{1,0:T(8,128)(2,1)} %copy-done.52, f32[576,768]{1,0:T(8,128)} %fusion.20, f32[768]{0:T(1024)} %convert_element_type.311, f32[768]{0:T(1024)S(1)} %copy-done.40, f32[576]{0:T(1024)} %copy-done.41, f32[576]{0:T(1024)S(1)} %copy-done.34), kind=kOutput, calls=%fused_computation.23 | convolution fusion | flops 2722480128 | bytes 10037760 | tf_op jit(solution)/shard_map/iqd,iqf->df/dot_general | solution.py:138
  233.3 24.4 %reduce-scatter.15.cloned.1.call-done = bf16[768,576]{0,1:T(8,128)(2,1)} async-done(((bf16[768,2304]{0,1:T(8,128)(2,1)}), bf16[768,576]{0,1:T(8,128)(2,1)}) %reduce-scatter.15.cloned.1.call-update) | async-done | bytes 884752 | tf_op jit(solution)/shard_map/reduce_scatter | solution.py:31
  260.5 47.8 %reduce-scatter.23.cloned.1.call-done = bf16[3072,192]{0,1:T(8,128)(2,1)} async-done(((bf16[3072,768]{0,1:T(8,128)(2,1)}), bf16[3072,192]{0,1:T(8,128)(2,1)}) %reduce-scatter.23.cloned.1.call-update) | async-done | bytes 1179664 | tf_op jit(solution)/shard_map/reduce_scatter | solution.py:31
  311.0 6.8 fusion.27
  320.9 8.0 %reduce.39 = bf16[576,768]{1,0:T(8,128)(2,1)} reduce(bf16[576,1,768]{2,1,0:T(2,128)(2,1)} %bitcast.128, bf16[]{:T(256)} %broadcast.360), dimensions={1}, to_apply=%bitcast.112.reduce_sub_computation | reduce | bytes 1769474
  332.4 4.3 all-to-all-start.2
  340.1 6.6 fusion.53
  346.7 21.3 %reduce-scatter.19.cloned.1.call-done = bf16[768,768]{1,0:T(8,128)(2,1)} async-done(((bf16[768,3072]{1,0:T(8,128)(2,1)}), bf16[768,768]{1,0:T(8,128)(2,1)}) %reduce-scatter.19.cloned.1.call-update) | async-done | bytes 1179664 | tf_op jit(solution)/shard_map/reduce_scatter | solution.py:31
  380.1 7.9 %reduce.40 = bf16[576,768]{1,0:T(8,128)(2,1)} reduce(bf16[576,1,768]{2,1,0:T(2,128)(2,1)} %bitcast.129, bf16[]{:T(256)} %broadcast.360), dimensions={1}, to_apply=%bitcast.111.reduce_sub_computation | reduce | bytes 1769474
  397.9 4.4 all-to-all-start.4
  407.2 26.1 %reduce-scatter.27.cloned.1.call-done = bf16[96,192]{1,0:T(8,128)(2,1)} async-done(((bf16[768,192]{1,0:T(8,128)(2,1)}), bf16[96,192]{1,0:T(8,128)(2,1)}) %reduce-scatter.27.cloned.1.call-update) | async-done | bytes 36880 | tf_op jit(solution)/shard_map/reduce_scatter | solution.py:32
  436.6 63.6 %reduce-scatter.25.cloned.1.call-done = bf16[96,576]{1,0:T(8,128)(2,1)} async-done(((bf16[768,576]{1,0:T(8,128)(2,1)}), bf16[96,576]{1,0:T(8,128)(2,1)}) %reduce-scatter.25.cloned.1.call-update) | async-done | bytes 110608 | tf_op jit(solution)/shard_map/reduce_scatter | solution.py:32
  503.2 41.3 %psum.7 = f32[10752]{0:T(1024)} all-reduce(f32[10752]{0:T(1024)} %constant_dynamic-update-slice_fusion), channel_id=1, replica_groups=mesh['img'=8,'band'=4] {'img','band'}, use_global_device_ids=true, to_apply=%region_21.22 | all-reduce | flops 10752 | bytes 86016 | tf_op jit(solution)/shard_map/psum | solution.py:193
  546.9 21.6 %reduce-scatter.29.cloned.1.call-done = bf16[384,192]{1,0:T(8,128)(2,1)} async-done(((bf16[3072,192]{1,0:T(8,128)(2,1)}), bf16[384,192]{1,0:T(8,128)(2,1)}) %reduce-scatter.29.cloned.1.call-update) | async-done | bytes 147472 | tf_op jit(solution)/shard_map/reduce_scatter | solution.py:32
  570.2 65.4 %reduce-scatter.21.cloned.1.call-done = bf16[96,768]{1,0:T(8,128)(2,1)} async-done(((bf16[768,768]{1,0:T(8,128)(2,1)}), bf16[96,768]{1,0:T(8,128)(2,1)}) %reduce-scatter.21.cloned.1.call-update) | async-done | bytes 147472 | tf_op jit(solution)/shard_map/reduce_scatter | solution.py:32
  (278 shorter events, 207.2 us)
Async XLA Ops:
  7.2 38.5 %copy-start = (bf16[768,2304]{1,0:T(8,128)(2,1)S(1)}, bf16[768,2304]{1,0:T(8,128)(2,1)}, u32[]{:S(2)}) copy-start(bf16[768,2304]{1,0:T(8,128)(2,1)} %param.22) | copy-start | bytes 10616836
  8.6 8.0 %all-to-all-start = ((s32[4,1,144]{2,1,0:T(1,128)}), s32[4,1,144]{2,1,0:T(1,128)S(1)}, u32[]{:S(2)}, u32[]{:S(2)}) async-start(s32[4,1,144]{2,1,0:T(1,128)} %all_to_all.17), calls=%async_computation | async-start | bytes 8192 | tf_op jit(solution)/shard_map/all_to_all | solution.py:85
  16.7 17.0 %all-to-all-start.1 = ((bf16[4,144,768]{2,1,0:T(8,128)(2,1)}), bf16[4,144,768]{2,1,0:T(8,128)(2,1)}, u32[]{:S(2)}, u32[]{:S(2)}) async-start(bf16[4,144,768]{2,1,0:T(8,128)(2,1)} %param.17), calls=%async_computation.1 | async-start | bytes 1769472 | tf_op jit(solution)/shard_map/all_to_all | solution.py:85
  33.7 88.2 %all-to-all-start.3 = ((bf16[4,144,768]{2,1,0:T(8,128)(2,1)}), bf16[4,144,768]{2,1,0:T(8,128)(2,1)}, u32[]{:S(2)}, u32[]{:S(2)}) async-start(bf16[4,144,768]{2,1,0:T(8,128)(2,1)} %param.33), calls=%async_computation.3 | async-start | bytes 1769472 | tf_op jit(solution)/shard_map/all_to_all | solution.py:85
  37.9 193.4 %reduce-scatter.17.cloned.1.call-start = ((), (), s32[]{:S(2)}) async-start(), calls=%async_computation.14 | async-start | bytes 1474560 | tf_op jit(solution)/shard_map/reduce_scatter | solution.py:31
  152.0 15.5 %copy-start.28 = (f32[12,576]{1,0:T(8,128)S(1)}, f32[12,576]{1,0:T(8,128)}, u32[]{:S(2)}) copy-start(f32[12,576]{1,0:T(8,128)} %get-tuple-element.97) | copy-start | bytes 82948
  167.5 12.3 %copy-start.3 = (bf16[1,576,12,32]{1,3,2,0:T(8,128)(2,1)S(1)}, bf16[1,576,12,32]{1,3,2,0:T(8,128)(2,1)}, u32[]{:S(2)}) copy-start(bf16[1,576,12,32]{1,3,2,0:T(8,128)(2,1)} %copy-done.2) | copy-start | bytes 1327108
  167.5 12.3 %copy-start.5 = (bf16[1,576,12,32]{1,3,2,0:T(8,128)(2,1)S(1)}, bf16[1,576,12,32]{1,3,2,0:T(8,128)(2,1)}, u32[]{:S(2)}) copy-start(bf16[1,576,12,32]{1,3,2,0:T(8,128)(2,1)} %copy-done.4) | copy-start | bytes 1327108
  186.8 70.9 %reduce-scatter.15.cloned.1.call-start = ((), (), s32[]{:S(2)}) async-start(), calls=%async_computation.13 | async-start | bytes 4423680 | tf_op jit(solution)/shard_map/reduce_scatter | solution.py:31
  212.8 95.5 %reduce-scatter.23.cloned.1.call-start = ((), (), s32[]{:S(2)}) async-start(), calls=%async_computation.17 | async-start | bytes 5898240 | tf_op jit(solution)/shard_map/reduce_scatter | solution.py:31
  221.4 146.6 %reduce-scatter.19.cloned.1.call-start = ((), (), s32[]{:S(2)}) async-start(), calls=%async_computation.15 | async-start | bytes 5898240 | tf_op jit(solution)/shard_map/reduce_scatter | solution.py:31
  231.3 202.1 %reduce-scatter.27.cloned.1.call-start = ((), (), s32[]{:S(2)}) async-start(), calls=%async_computation.19 | async-start | bytes 442368 | tf_op jit(solution)/shard_map/reduce_scatter | solution.py:32
  233.3 267.0 %reduce-scatter.25.cloned.1.call-start = ((), (), s32[]{:S(2)}) async-start(), calls=%async_computation.18 | async-start | bytes 1105920 | tf_op jit(solution)/shard_map/reduce_scatter | solution.py:32
  260.0 50.9 %copy-start.48 = (bf16[768]{0:T(1024)(128)(2,1)S(1)}, bf16[768]{0:T(1024)(128)(2,1)}, u32[]{:S(2)}) copy-start(bf16[768]{0:T(1024)(128)(2,1)} %param.32) | copy-start | bytes 4612
  260.0 308.5 %reduce-scatter.29.cloned.1.call-start = ((), (), s32[]{:S(2)}) async-start(), calls=%async_computation.20 | async-start | bytes 1769472 | tf_op jit(solution)/shard_map/reduce_scatter | solution.py:32
  332.4 65.4 %all-to-all-start.2 = ((bf16[4,2,55296]{2,1,0:T(2,128)(2,1)}), bf16[4,2,55296]{2,1,0:T(2,128)(2,1)}, u32[]{:S(2)}, u32[]{:S(2)}) async-start(bf16[4,2,55296]{2,1,0:T(2,128)(2,1)} %reshape.785), calls=%async_computation.2 | async-start | bytes 1769472 | tf_op jit(solution)/shard_map/all_to_all | solution.py:88
  336.8 298.8 %reduce-scatter.21.cloned.1.call-start = ((), (), s32[]{:S(2)}) async-start(), calls=%async_computation.16 | async-start | bytes 1327104 | tf_op jit(solution)/shard_map/reduce_scatter | solution.py:32
  380.1 12.6 %copy-start.47 = (f32[768]{0:T(1024)S(1)}, f32[768]{0:T(1024)}, u32[]{:S(2)}) copy-start(f32[768]{0:T(1024)} %get-tuple-element.65) | copy-start | bytes 9220
  380.1 13.9 %copy-start.27 = (f32[576]{0:T(1024)S(1)}, f32[576]{0:T(1024)}, u32[]{:S(2)}) copy-start(f32[576]{0:T(1024)} %get-tuple-element.108) | copy-start | bytes 6916
  397.9 255.6 %all-to-all-start.4 = ((bf16[4,2,55296]{2,1,0:T(2,128)(2,1)}), bf16[4,2,55296]{2,1,0:T(2,128)(2,1)}, u32[]{:S(2)}, u32[]{:S(2)}) async-start(bf16[4,2,55296]{2,1,0:T(2,128)(2,1)} %reshape.787), calls=%async_computation.4 | async-start | bytes 1769472 | tf_op jit(solution)/shard_map/all_to_all | solution.py:88
  434.9 109.6 %collective-permute-start.3 = (bf16[96,192]{0,1:T(8,128)(2,1)}, bf16[96,192]{0,1:T(8,128)(2,1)}, u32[]{:S(2)}, u32[]{:S(2)}) collective-permute-start(bf16[96,192]{0,1:T(8,128)(2,1)} %copy.124), channel_id=1, source_target_pairs={{0,1},{1,2},{2,3},{3,0},{4,5},{5,6},{6,7},{7,4},{8,9},{9,10},{10,1... | collective-permute-start | bytes 110600 | tf_op jit(solution)/shard_map/ppermute | solution.py:42
  434.9 135.4 %collective-permute-start.4 = (bf16[96,192]{0,1:T(8,128)(2,1)}, bf16[96,192]{0,1:T(8,128)(2,1)}, u32[]{:S(2)}, u32[]{:S(2)}) collective-permute-start(bf16[96,192]{0,1:T(8,128)(2,1)} %copy.124), channel_id=1, source_target_pairs={{0,3},{1,0},{2,1},{3,2},{4,7},{5,4},{6,5},{7,6},{8,11},{9,8},{10,9... | collective-permute-start | bytes 110600 | tf_op jit(solution)/shard_map/ppermute | solution.py:47
  501.9 44.3 %collective-permute-start = (bf16[96,576]{0,1:T(8,128)(2,1)}, bf16[96,576]{0,1:T(8,128)(2,1)}, u32[]{:S(2)}, u32[]{:S(2)}) collective-permute-start(bf16[96,576]{0,1:T(8,128)(2,1)} %copy.122), channel_id=1, source_target_pairs={{0,1},{1,2},{2,3},{3,0},{4,5},{5,6},{6,7},{7,4},{8,9},{9,10},{10,1... | collective-permute-start | bytes 331784 | tf_op jit(solution)/shard_map/ppermute | solution.py:42
  544.5 123.9 %collective-permute-start.5 = (bf16[96,192]{0,1:T(8,128)(2,1)}, bf16[96,192]{0,1:T(8,128)(2,1)}, u32[]{:S(2)}, u32[]{:S(2)}) collective-permute-start(bf16[96,192]{0,1:T(8,128)(2,1)} %collective-permute-done.3), channel_id=1, source_target_pairs={{0,1},{1,2},{2,3},{3,0},{4,5},{5,6},{6,7},{7,4},{8,9},{9,10},{10,1... | collective-permute-start | bytes 110600 | tf_op jit(solution)/shard_map/ppermute | solution.py:42
  544.5 134.6 %collective-permute-start.1 = (bf16[96,576]{0,1:T(8,128)(2,1)}, bf16[96,576]{0,1:T(8,128)(2,1)}, u32[]{:S(2)}, u32[]{:S(2)}) collective-permute-start(bf16[96,576]{0,1:T(8,128)(2,1)} %copy.122), channel_id=1, source_target_pairs={{0,3},{1,0},{2,1},{3,2},{4,7},{5,4},{6,5},{7,6},{8,11},{9,8},{10,9... | collective-permute-start | bytes 331784 | tf_op jit(solution)/shard_map/ppermute | solution.py:47
  546.2 136.6 %collective-permute-start.2 = (bf16[96,576]{0,1:T(8,128)(2,1)}, bf16[96,576]{0,1:T(8,128)(2,1)}, u32[]{:S(2)}, u32[]{:S(2)}) collective-permute-start(bf16[96,576]{0,1:T(8,128)(2,1)} %collective-permute-done), channel_id=1, source_target_pairs={{0,1},{1,2},{2,3},{3,0},{4,5},{5,6},{6,7},{7,4},{8,9},{9,10},{10,1... | collective-permute-start | bytes 331784 | tf_op jit(solution)/shard_map/ppermute | solution.py:42
  570.2 125.6 %collective-permute-start.9 = (bf16[384,192]{0,1:T(8,128)(2,1)}, bf16[384,192]{0,1:T(8,128)(2,1)}, u32[]{:S(2)}, u32[]{:S(2)}) collective-permute-start(bf16[384,192]{0,1:T(8,128)(2,1)} %copy.126), channel_id=1, source_target_pairs={{0,1},{1,2},{2,3},{3,0},{4,5},{5,6},{6,7},{7,4},{8,9},{9,10},{10,1... | collective-permute-start | bytes 442376 | tf_op jit(solution)/shard_map/ppermute | solution.py:42
  635.6 61.1 %collective-permute-start.6 = (bf16[96,768]{1,0:T(8,128)(2,1)}, bf16[96,768]{1,0:T(8,128)(2,1)}, u32[]{:S(2)}, u32[]{:S(2)}) collective-permute-start(bf16[96,768]{1,0:T(8,128)(2,1)} %reduce-scatter.21.cloned.1.call-done), channel_id=1, source_target_pairs={{0,1},{1,2},{2,3},{3,0},{4,5},{5,6},{6,7},{7,4},{8,9},{9,10},{10,1... | collective-permute-start | bytes 442376 | tf_op jit(solution)/shard_map/ppermute | solution.py:42
  688.3 15.4 %collective-permute-start.10 = (bf16[384,192]{0,1:T(8,128)(2,1)}, bf16[384,192]{0,1:T(8,128)(2,1)}, u32[]{:S(2)}, u32[]{:S(2)}) collective-permute-start(bf16[384,192]{0,1:T(8,128)(2,1)} %copy.126), channel_id=1, source_target_pairs={{0,3},{1,0},{2,1},{3,2},{4,7},{5,4},{6,5},{7,6},{8,11},{9,8},{10,9... | collective-permute-start | bytes 442376 | tf_op jit(solution)/shard_map/ppermute | solution.py:47
  690.1 19.0 %collective-permute-start.7 = (bf16[96,768]{1,0:T(8,128)(2,1)}, bf16[96,768]{1,0:T(8,128)(2,1)}, u32[]{:S(2)}, u32[]{:S(2)}) collective-permute-start(bf16[96,768]{1,0:T(8,128)(2,1)} %reduce-scatter.21.cloned.1.call-done), channel_id=1, source_target_pairs={{0,3},{1,0},{2,1},{3,2},{4,7},{5,4},{6,5},{7,6},{8,11},{9,8},{10,9... | collective-permute-start | bytes 442376 | tf_op jit(solution)/shard_map/ppermute | solution.py:47
  695.8 14.9 %collective-permute-start.11 = (bf16[384,192]{0,1:T(8,128)(2,1)}, bf16[384,192]{0,1:T(8,128)(2,1)}, u32[]{:S(2)}, u32[]{:S(2)}) collective-permute-start(bf16[384,192]{0,1:T(8,128)(2,1)} %collective-permute-done.9), channel_id=1, source_target_pairs={{0,1},{1,2},{2,3},{3,0},{4,5},{5,6},{6,7},{7,4},{8,9},{9,10},{10,1... | collective-permute-start | bytes 442376 | tf_op jit(solution)/shard_map/ppermute | solution.py:42
  696.7 21.2 %collective-permute-start.8 = (bf16[96,768]{1,0:T(8,128)(2,1)}, bf16[96,768]{1,0:T(8,128)(2,1)}, u32[]{:S(2)}, u32[]{:S(2)}) collective-permute-start(bf16[96,768]{1,0:T(8,128)(2,1)} %collective-permute-done.6), channel_id=1, source_target_pairs={{0,1},{1,2},{2,3},{3,0},{4,5},{5,6},{6,7},{7,4},{8,9},{9,10},{10,1... | collective-permute-start | bytes 442376 | tf_op jit(solution)/shard_map/ppermute | solution.py:42
  (46 other events, 207.8 us)
Sparse Core Ops, SparseCore 0:
  186.9 27.8 reduce-scatter.16
  217.4 40.3 reduce-scatter.14
  260.3 47.9 reduce-scatter.22
  310.7 57.2 reduce-scatter.18
  371.1 62.1 reduce-scatter.26
  437.1 63.0 reduce-scatter.24
  503.7 64.8 reduce-scatter.28
  571.9 63.6 reduce-scatter.20
